TPU v7x, 128 devices: a whole 4x4x4 slice. The times are simulated.
128 devices in a mesh: ctx: 32 (over x, y_lo, z), head: 4 (over y_hi, core).
Axes of the slice: x: 4, y: 4 (y_hi: 2, y_lo: 2; y = y_hi * 2 + y_lo), z: 4, core: 2. Of those that a mesh axis runs over, the one named last changes fastest.
Arguments:
- queries: bfloat16 [32768, 1024], P('ctx', 'head'), may hold values from -18 to 18
- keys: bfloat16 [32768, 128], P('ctx'), may hold values from -6 to 6
- values: bfloat16 [32768, 128], P('ctx'), may hold values from -6 to 6
- grad_out: bfloat16 [32768, 1024], P('ctx', 'head'), may hold values from -6 to 6
- lengths: int32 [128], replicated, may hold values from 1 to 4096, 32768 in all
Outputs:
- attn_out: bfloat16 [32768, 1024], P('ctx', 'head')
- grad_queries: bfloat16 [32768, 1024], P('ctx', 'head')
- grad_keys: bfloat16 [32768, 128], P(('ctx', 'head'))
- grad_values: bfloat16 [32768, 128], P(('ctx', 'head'))
Inputs may be any that keep to these rules, and one draw needn't show every extreme that they name: The lengths sum to 32768; one response has exactly 4096 tokens.
All inputs are finite; a program needn't handle non-finite values.
Results may differ from a plain program's by a relative error of at most 0.0072.
Values may be sent and summed in bfloat16 or wider, within the bound.
No kernel may reach another device: no remote copies, remote signals or barrier semaphores. Data moves between devices by JAX's collectives and lax.ppermute only.
A program may use at most 192 MiB of HBM per device.

v0:
```python
from functools import partial
import math

import jax
import jax.numpy as jnp
from jax import lax
from jax.sharding import PartitionSpec as P

DH = 128
SPAN = 4


masked_score = -1e30


def passed_along(x, axis, by):
    count = lax.axis_size(axis)
    pairs = [(i, i + by) for i in range(count) if 0 <= i + by < count]
    return lax.ppermute(x, axis, pairs)


def in_blocks(x, dim, count):
    dims = x.shape
    tiles = x.reshape(*dims[:dim], count, dims[dim] // count, *dims[dim + 1 :])
    return jnp.moveaxis(tiles, dim, 0)


def sent_and_summed(x, axis, dim):
    tiles = in_blocks(x, dim, lax.axis_size(axis))
    arrived = lax.all_to_all(tiles, axis, split_axis=0, concat_axis=0, tiled=True)
    return arrived.sum(axis=0)


def side_by_side(arrays, axis, dim, along):
    widths = [a.shape[along] for a in arrays]
    both = jnp.concatenate(arrays, axis=along)
    whole = sent_and_summed(both, axis, dim)
    return tuple(jnp.split(whole, [sum(widths[:k]) for k in range(1, len(widths))], axis=along))


def row_info(positions, cumulative):
    before = cumulative[None, :] <= positions[:, None]
    doc_ids = jnp.sum(before.astype(jnp.int32), axis=1)
    begins = jnp.max(jnp.where(before, cumulative[None, :], 0), axis=1)
    return (doc_ids, begins)


def block_scores(query_block, query_pos, query_doc, kmatrix, key_pos, key_doc):
    scaled = jnp.einsum("qhd,kd->hqk", query_block, kmatrix, preferred_element_type=jnp.float32) * (
        1.0 / math.sqrt(kmatrix.shape[1])
    )
    visible = (query_doc[:, None] == key_doc[None, :]) & (key_pos[None, :] <= query_pos[:, None])
    return jnp.where(visible[None], scaled, masked_score)


def guarded(needed, compute, blank_fn):
    if needed is None:
        return compute()
    return lax.cond(needed, compute, blank_fn)


def forward_piece(scores, row_lse, vmatrix):
    probs_low = jnp.exp(scores - row_lse[..., None]).astype(jnp.bfloat16)
    return jnp.einsum("hqk,kd->qhd", probs_low, vmatrix, preferred_element_type=jnp.float32)


def backward_piece(
    scores, row_lse, delta, query_block, grad_block, kmatrix, vmatrix, key_acc, value_acc
):
    factor = 1.0 / math.sqrt(kmatrix.shape[1])
    probs = jnp.exp(scores - row_lse[..., None])
    probs_low = probs.astype(jnp.bfloat16)
    dprob = jnp.einsum("qhd,kd->hqk", grad_block, vmatrix, preferred_element_type=jnp.float32)
    dscore = (probs * (dprob - delta[..., None])).astype(jnp.bfloat16)
    query_grad = (
        jnp.einsum("hqk,kd->qhd", dscore, kmatrix, preferred_element_type=jnp.float32) * factor
    )
    key_acc = (
        key_acc
        + jnp.einsum("hqk,qhd->kd", dscore, query_block, preferred_element_type=jnp.float32)
        * factor
    )
    value_acc = value_acc + jnp.einsum(
        "hqk,qhd->kd", probs_low, grad_block, preferred_element_type=jnp.float32
    )
    return (query_grad, key_acc, value_acc)


def keep_grads(shape, key_acc, value_acc):
    return (jnp.zeros(shape, jnp.float32), key_acc, value_acc)


def attend(query_rows, grad_rows, query_pos, query_doc, pieces):
    row_total = query_rows.shape[0]
    head_count = query_rows.shape[1] // DH
    block_rows = min(row_total, 512)
    block_count = row_total // block_rows
    blocks = (
        query_rows.reshape(block_count, block_rows, head_count, DH),
        grad_rows.reshape(block_count, block_rows, head_count, DH),
        query_pos.reshape(block_count, block_rows),
        query_doc.reshape(block_count, block_rows),
    )
    out_shape = (block_rows, head_count, DH)

    def per_block(grad_state, block_in):
        query_block, grad_block, block_pos, block_doc = block_in
        flags = []
        score_list = []
        for piece_index, piece in enumerate(pieces):
            kmatrix, vmatrix, key_pos, key_doc = piece
            compute = partial(
                block_scores, query_block, block_pos, block_doc, kmatrix, key_pos, key_doc
            )
            blank_fn = partial(
                jnp.full, (head_count, block_rows, kmatrix.shape[0]), masked_score, jnp.float32
            )
            needed = None
            if piece_index > 0:
                needed = (key_pos[0] >= 0) & (block_doc[0] == key_doc[-1])
            flags.append(needed)
            score_list.append(guarded(needed, compute, blank_fn))
        highest = jnp.max(score_list[0], axis=2)
        for scores in score_list[1:]:
            highest = jnp.maximum(highest, jnp.max(scores, axis=2))
        exp_total = jnp.zeros_like(highest)
        for scores in score_list:
            exp_total = exp_total + jnp.sum(jnp.exp(scores - highest[..., None]), axis=2)
        row_lse = highest + jnp.log(exp_total)
        out32 = jnp.zeros(out_shape, jnp.float32)
        for needed, scores, piece in zip(flags, score_list, pieces):
            out32 = out32 + guarded(
                needed,
                partial(forward_piece, scores, row_lse, piece[1]),
                partial(jnp.zeros, out_shape, jnp.float32),
            )
        delta = jnp.sum(grad_block.astype(jnp.float32) * out32, axis=2).T
        query_total = jnp.zeros(out_shape, jnp.float32)
        new_state = []
        for needed, scores, piece, grad_pair in zip(flags, score_list, pieces, grad_state):
            result = guarded(
                needed,
                partial(
                    backward_piece,
                    scores,
                    row_lse,
                    delta,
                    query_block,
                    grad_block,
                    piece[0],
                    piece[1],
                    grad_pair[0],
                    grad_pair[1],
                ),
                partial(keep_grads, out_shape, grad_pair[0], grad_pair[1]),
            )
            query_total = query_total + result[0]
            new_state.append((result[1], result[2]))
        return (tuple(new_state), (out32.astype(jnp.bfloat16), query_total.astype(jnp.bfloat16)))

    start_state = tuple(
        (
            (
                jnp.zeros((piece[0].shape[0], DH), jnp.float32),
                jnp.zeros((piece[0].shape[0], DH), jnp.float32),
            )
            for piece in pieces
        )
    )
    final_state, (outputs, query_grads) = lax.scan(per_block, start_state, blocks)
    return (
        outputs.reshape(row_total, head_count * DH),
        query_grads.reshape(row_total, head_count * DH),
        tuple((pair[0] for pair in final_state)),
        tuple((pair[1] for pair in final_state)),
    )


def shards(queries, keys, values, grad_out, lengths):
    row_count = queries.shape[0]
    place = lax.axis_index("ctx")
    cumulative = jnp.cumsum(lengths)
    offsets = jnp.arange(row_count, dtype=jnp.int32)

    def positions_of(shard):
        return shard * row_count + offsets

    own_pos = positions_of(place)
    own_doc, own_begin = row_info(own_pos, cumulative)
    pieces = [(keys, values, own_pos, own_doc)]
    for distance in range(1, SPAN + 1):
        arrived = passed_along((keys, values), "ctx", distance)
        key_pos = positions_of(place - distance)
        key_doc = row_info(key_pos, cumulative)[0]
        pieces.append((arrived[0], arrived[1], key_pos, key_doc))
    whole_part = attend(queries, grad_out, own_pos, own_doc, pieces)
    attn_out = whole_part[0]
    grad_queries = whole_part[1]
    key_parts = list(whole_part[2])
    value_parts = list(whole_part[3])
    key_total = key_parts[0]
    value_total = value_parts[0]
    for distance in range(1, SPAN + 1):
        back_parts = passed_along((key_parts[distance], value_parts[distance]), "ctx", -distance)
        key_total = key_total + back_parts[0]
        value_total = value_total + back_parts[1]
    key_share, value_share = side_by_side((key_total, value_total), "head", 0, 1)
    return (
        attn_out,
        grad_queries,
        key_share.astype(jnp.bfloat16),
        value_share.astype(jnp.bfloat16),
    )


def solution(mesh):
    placed = (P("ctx", "head"), P("ctx", None), P("ctx", None), P("ctx", "head"), P())
    return jax.shard_map(
        shards,
        mesh=mesh,
        in_specs=placed,
        out_specs=(
            P("ctx", "head"),
            P("ctx", "head"),
            P(("ctx", "head"), None),
            P(("ctx", "head"), None),
        ),
        check_vma=False,
    )
```

profile of v0, /device:TPU:12, one launch (start us, length us, event | category | flops | bytes accessed | tf_op | source)
XLA Modules:
  0.0 493.1 jit_solution(8545204426051852044)
XLA Ops:
  0.6 3.8 collective-permute-start
  4.5 5.5 %collective-permute-start.1 = (bf16[1024,128]{1,0:T(8,128)(2,1)}, bf16[1024,128]{1,0:T(8,128)(2,1)}, u32[]{:S(2)}, u32[]{:S(2)}) collective-permute-start(bf16[1024,128]{1,0:T(8,128)(2,1)} %param.32), channel_id=1, source_target_pairs={{0,8},{4,12},{8,16},{12,20},{16,24},{20,28},{24,32},{28,36},{32,40... | collective-permute-start | bytes 786440 | tf_op jit(solution)/shard_map/ppermute | solution.py:19
  10.0 3.4 collective-permute-start.2
  13.4 3.5 collective-permute-start.3
  22.3 3.6 collective-permute-start.6
  48.3 264.9 %while.34 = (s32[]{:T(128)}, f32[1024,128]{1,0:T(8,128)}, f32[1024,128]{1,0:T(8,128)}, f32[1024,128]{1,0:T(8,128)}, f32[1024,128]{1,0:T(8,128)}, /*index=5*/f32[...) while((s32[]{:T(128)}, f32[1024,128]{1,0:T(8,128)}, ...), condition=%wide.region_42.43_spmd.clone, body=%wide.region_6.42_spmd.clone.sunk | while | flops 8142069760 | bytes 288470976 | solution.py:170
  75.7 11.4 %conditional.36 = (f32[2,512,1024]{1,2,0:T(8,128)}, f32[2,512]{1,0:T(2,128)}, f32[2,512,1]{1,0,2:T(2,128)S(1)}, f32[2,512,1024]{2,1,0:T(8,128)}) conditional(s32[]{:T(128)} %convert_element_type.186, () %tuple.227, (s32[512]{0:T(512)S(1)}, s32[1024]{0:T(1024)S(1)}, s32[]{:T(128)}, s32[512]{0:T(512)S(1)}, bf16[1024,128]{1,0:T(8,128)(2,1)}, ...), branch_computations={%region_17.17_spmd, %region_18.19_spmd} | conditional | flops 273154048 | bytes 14188580 | solution.py:59
  76.5 4.4 fusion.132
  81.0 5.4 %copy.89 = f32[2,512,1024]{2,1,0:T(8,128)} copy(f32[2,512,1024]{1,2,0:T(8,128)} %get-tuple-element.1462) | data formatting | bytes 8388608 | tf_op jit(solution)/shard_map/while/body/eval_jaxpr/cond | solution.py:59
  88.9 11.4 %conditional.37 = (f32[2,512,1024]{1,2,0:T(8,128)}, f32[2,512]{1,0:T(2,128)}, f32[2,512,1]{1,0,2:T(2,128)S(1)}, f32[2,512,1024]{2,1,0:T(8,128)}) conditional(s32[]{:T(128)} %convert_element_type.187, () %tuple.229, (s32[512]{0:T(512)S(1)}, s32[1024]{0:T(1024)S(1)}, s32[]{:T(128)}, s32[512]{0:T(512)S(1)}, bf16[1024,128]{1,0:T(8,128)(2,1)}, ...), branch_computations={%region_14.14_spmd, %region_15.16_spmd} | conditional | flops 273154048 | bytes 14188580 | solution.py:59
  89.8 4.5 fusion.131
  94.3 5.4 %copy.87 = f32[2,512,1024]{2,1,0:T(8,128)} copy(f32[2,512,1024]{1,2,0:T(8,128)} %get-tuple-element.1470) | data formatting | bytes 8388608 | tf_op jit(solution)/shard_map/while/body/eval_jaxpr/cond | solution.py:59
  102.3 11.4 %conditional.38 = (f32[2,512,1024]{1,2,0:T(8,128)}, f32[2,512]{1,0:T(2,128)}, f32[2,512,1]{1,0,2:T(2,128)S(1)}, f32[2,512,1024]{2,1,0:T(8,128)}) conditional(s32[]{:T(128)} %convert_element_type.188, () %tuple.231, (s32[512]{0:T(512)S(1)}, s32[1024]{0:T(1024)S(1)}, s32[]{:T(128)}, s32[512]{0:T(512)S(1)}, bf16[1024,128]{1,0:T(8,128)(2,1)}, ...), branch_computations={%region_11.11_spmd, %region_12.13_spmd} | conditional | flops 273154048 | bytes 14188580 | solution.py:59
  103.2 4.4 fusion.130
  107.6 5.4 %copy.85 = f32[2,512,1024]{2,1,0:T(8,128)} copy(f32[2,512,1024]{1,2,0:T(8,128)} %get-tuple-element.1478) | data formatting | bytes 8388608 | tf_op jit(solution)/shard_map/while/body/eval_jaxpr/cond | solution.py:59
  115.5 11.4 %conditional.39 = (f32[2,512,1024]{1,2,0:T(8,128)}, f32[2,512]{1,0:T(2,128)}, f32[2,512,1]{1,0,2:T(2,128)S(1)}, f32[2,512,1024]{2,1,0:T(8,128)}) conditional(s32[]{:T(128)} %convert_element_type.189, () %tuple.233, (s32[512]{0:T(512)S(1)}, s32[1024]{0:T(1024)S(1)}, s32[]{:T(128)}, s32[512]{0:T(512)S(1)}, bf16[1024,128]{1,0:T(8,128)(2,1)}, ...), branch_computations={%region_8.8_spmd, %region_9.10_spmd} | conditional | flops 273154048 | bytes 14188580 | solution.py:59
  116.4 4.5 fusion.129
  120.9 5.4 %copy.83 = f32[2,512,1024]{2,1,0:T(8,128)} copy(f32[2,512,1024]{1,2,0:T(8,128)} %get-tuple-element.1486) | data formatting | bytes 8388608 | tf_op jit(solution)/shard_map/while/body/eval_jaxpr/cond | solution.py:59
  129.6 9.2 %exponential_reduce_fusion.5 = (f32[2,512]{1,0:T(2,128)S(1)}, f32[2,512]{1,0:T(2,128)S(1)}, f32[2,512]{1,0:T(2,128)S(1)}, f32[2,512]{1,0:T(2,128)S(1)}, f32[2,512]{1,0:T(2,128)S(1)}) fusion(f32[2,512,1024]{2,1,0:T(8,128)} %get-tuple-element.1423, f32[2,512]{1,0:T(2,128)S(1)} %bitcast.403, f32[2,512,1024]{2,1,0:T(8,128)} %get-tuple-element.1424, ...), kind=kLoop, calls=%fused_computation.117.clone.1 | loop fusion | flops 12577792 | bytes 21520384 | tf_op jit(solution)/shard_map/while/body/eval_jaxpr/reduce_sum | solution.py:128
  139.6 8.4 %conditional.43 = (f32[512,2,128]{2,0,1:T(8,128)S(1)}) conditional(s32[]{:T(128)} %convert_element_type.189, () %tuple.240, (f32[2,512]{1,0:T(2,128)S(1)}, f32[2,512,1024]{1,2,0:T(8,128)}, bf16[1024,128]{1,0:T(8,128)(2,1)}) %tuple.241), branch_computations={%region_25.25_spmd, %region_26.26_spmd} | conditional | flops 270532608 | bytes 13373448 | solution.py:59
  139.6 5.4 %copy.61 = f32[2,512,1024]{2,1,0:T(8,128)} copy(f32[2,512,1024]{1,2,0:T(8,128)} %get-tuple-element.947) | data formatting | bytes 8388608 | tf_op jit(solution)/shard_map
  145.0 3.0 fusion.16
  148.0 8.4 %conditional.42 = (f32[512,2,128]{2,0,1:T(8,128)S(1)}) conditional(s32[]{:T(128)} %convert_element_type.188, () %tuple.238, (f32[2,512]{1,0:T(2,128)S(1)}, f32[2,512,1024]{1,2,0:T(8,128)}, bf16[1024,128]{1,0:T(8,128)(2,1)}) %tuple.239), branch_computations={%region_27.27_spmd, %region_28.28_spmd} | conditional | flops 270532608 | bytes 13373448 | solution.py:59
  148.0 5.4 %copy.62 = f32[2,512,1024]{2,1,0:T(8,128)} copy(f32[2,512,1024]{1,2,0:T(8,128)} %get-tuple-element.950) | data formatting | bytes 8388608 | tf_op jit(solution)/shard_map
  153.4 3.0 fusion.20
  156.4 9.2 %conditional.41 = (f32[512,2,128]{2,0,1:T(8,128)}) conditional(s32[]{:T(128)} %convert_element_type.187, () %tuple.236, (f32[2,512]{1,0:T(2,128)S(1)}, f32[2,512,1024]{1,2,0:T(8,128)}, bf16[1024,128]{1,0:T(8,128)(2,1)}) %tuple.237), branch_computations={%region_29.29_spmd, %region_30.30_spmd} | conditional | flops 270532608 | bytes 13373448 | solution.py:59
  156.4 5.4 %copy.63 = f32[2,512,1024]{2,1,0:T(8,128)} copy(f32[2,512,1024]{1,2,0:T(8,128)} %get-tuple-element.953) | data formatting | bytes 8388608 | tf_op jit(solution)/shard_map
  161.8 3.8 fusion.24
  165.6 9.2 %conditional.40 = (f32[512,2,128]{2,0,1:T(8,128)}) conditional(s32[]{:T(128)} %convert_element_type.186, () %tuple.226, (f32[2,512]{1,0:T(2,128)S(1)}, f32[2,512,1024]{1,2,0:T(8,128)}, bf16[1024,128]{1,0:T(8,128)(2,1)}) %tuple.235), branch_computations={%region_31.31_spmd, %region_32.32_spmd} | conditional | flops 270532608 | bytes 13373448 | solution.py:59
  165.6 5.4 %copy.64 = f32[2,512,1024]{2,1,0:T(8,128)} copy(f32[2,512,1024]{1,2,0:T(8,128)} %get-tuple-element.956) | data formatting | bytes 8388608 | tf_op jit(solution)/shard_map
  171.0 3.8 fusion.28
  175.9 4.6 convert_bitcast_fusion.2
  180.6 11.3 %conditional.47 = (f32[512,2,128]{2,0,1:T(8,128)S(1)}, f32[1024,128]{1,0:T(8,128)}, f32[1024,128]{1,0:T(8,128)}) conditional(s32[]{:T(128)} %convert_element_type.186, (f32[1024,128]{1,0:T(8,128)}, f32[1024,128]{1,0:T(8,128)}) %tuple.248, (f32[2,512]{1,0:T(2,128)S(1)}, f32[2,512,1024]{1,2,0:T(8,128)}, bf16[1024,128]{1,0:T(8,128)(2,1)}, ...), branch_computations={%region_40.40_spmd, %region_41.41_spmd} | conditional | flops 1080557568 | bytes 18624536 | solution.py:59
  180.6 3.2 fusion.82
  188.0 3.8 fusion.93
  191.9 11.2 %conditional.46 = (f32[512,2,128]{2,0,1:T(8,128)S(1)}, f32[1024,128]{1,0:T(8,128)}, f32[1024,128]{1,0:T(8,128)}) conditional(s32[]{:T(128)} %convert_element_type.187, (f32[1024,128]{1,0:T(8,128)}, f32[1024,128]{1,0:T(8,128)}) %tuple.246, (f32[2,512]{1,0:T(2,128)S(1)}, f32[2,512,1024]{1,2,0:T(8,128)}, bf16[1024,128]{1,0:T(8,128)(2,1)}, ...), branch_computations={%region_38.38_spmd, %region_39.39_spmd} | conditional | flops 1080557568 | bytes 18624536 | solution.py:59
  191.9 3.1 fusion.65
  199.3 3.8 fusion.76
  204.0 11.3 %conditional.45 = (f32[512,2,128]{2,0,1:T(8,128)S(1)}, f32[1024,128]{1,0:T(8,128)}, f32[1024,128]{1,0:T(8,128)}) conditional(s32[]{:T(128)} %convert_element_type.188, (f32[1024,128]{1,0:T(8,128)}, f32[1024,128]{1,0:T(8,128)}) %tuple.244, (f32[2,512]{1,0:T(2,128)S(1)}, f32[2,512,1024]{1,2,0:T(8,128)}, bf16[1024,128]{1,0:T(8,128)(2,1)}, ...), branch_computations={%region_36.36_spmd, %region_37.37_spmd} | conditional | flops 1080557568 | bytes 18624536 | solution.py:59
  204.0 3.2 fusion.48
  211.4 3.9 fusion.59
  216.1 11.3 %conditional.44 = (f32[512,2,128]{2,0,1:T(8,128)S(1)}, f32[1024,128]{1,0:T(8,128)}, f32[1024,128]{1,0:T(8,128)}) conditional(s32[]{:T(128)} %convert_element_type.189, (f32[1024,128]{1,0:T(8,128)}, f32[1024,128]{1,0:T(8,128)}) %tuple.242, (f32[2,512]{1,0:T(2,128)S(1)}, f32[2,512,1024]{1,2,0:T(8,128)}, bf16[1024,128]{1,0:T(8,128)(2,1)}, ...), branch_computations={%region_34.34_spmd, %region_35.35_spmd} | conditional | flops 1080557568 | bytes 18624536 | solution.py:59
  216.1 3.1 fusion.31
  223.5 3.8 fusion.42
  228.1 3.9 fusion.186
  236.1 4.4 fusion.188
  245.8 5.7 %conditional.36 = (f32[2,512,1024]{1,2,0:T(8,128)}, f32[2,512]{1,0:T(2,128)}, f32[2,512,1]{1,0,2:T(2,128)S(1)}, f32[2,512,1024]{2,1,0:T(8,128)}) conditional(s32[]{:T(128)} %convert_element_type.186, () %tuple.227, (s32[512]{0:T(512)S(1)}, s32[1024]{0:T(1024)S(1)}, s32[]{:T(128)}, s32[512]{0:T(512)S(1)}, bf16[1024,128]{1,0:T(8,128)(2,1)}, ...), branch_computations={%region_17.17_spmd, %region_18.19_spmd} | conditional | flops 273154048 | bytes 14188580 | solution.py:59
  253.4 5.6 %conditional.37 = (f32[2,512,1024]{1,2,0:T(8,128)}, f32[2,512]{1,0:T(2,128)}, f32[2,512,1]{1,0,2:T(2,128)S(1)}, f32[2,512,1024]{2,1,0:T(8,128)}) conditional(s32[]{:T(128)} %convert_element_type.187, () %tuple.229, (s32[512]{0:T(512)S(1)}, s32[1024]{0:T(1024)S(1)}, s32[]{:T(128)}, s32[512]{0:T(512)S(1)}, bf16[1024,128]{1,0:T(8,128)(2,1)}, ...), branch_computations={%region_14.14_spmd, %region_15.16_spmd} | conditional | flops 273154048 | bytes 14188580 | solution.py:59
  260.9 5.5 %conditional.38 = (f32[2,512,1024]{1,2,0:T(8,128)}, f32[2,512]{1,0:T(2,128)}, f32[2,512,1]{1,0,2:T(2,128)S(1)}, f32[2,512,1024]{2,1,0:T(8,128)}) conditional(s32[]{:T(128)} %convert_element_type.188, () %tuple.231, (s32[512]{0:T(512)S(1)}, s32[1024]{0:T(1024)S(1)}, s32[]{:T(128)}, s32[512]{0:T(512)S(1)}, bf16[1024,128]{1,0:T(8,128)(2,1)}, ...), branch_computations={%region_11.11_spmd, %region_12.13_spmd} | conditional | flops 273154048 | bytes 14188580 | solution.py:59
  268.4 5.6 %conditional.39 = (f32[2,512,1024]{1,2,0:T(8,128)}, f32[2,512]{1,0:T(2,128)}, f32[2,512,1]{1,0,2:T(2,128)S(1)}, f32[2,512,1024]{2,1,0:T(8,128)}) conditional(s32[]{:T(128)} %convert_element_type.189, () %tuple.233, (s32[512]{0:T(512)S(1)}, s32[1024]{0:T(1024)S(1)}, s32[]{:T(128)}, s32[512]{0:T(512)S(1)}, bf16[1024,128]{1,0:T(8,128)(2,1)}, ...), branch_computations={%region_8.8_spmd, %region_9.10_spmd} | conditional | flops 273154048 | bytes 14188580 | solution.py:59
  276.6 9.2 %exponential_reduce_fusion.5 = (f32[2,512]{1,0:T(2,128)S(1)}, f32[2,512]{1,0:T(2,128)S(1)}, f32[2,512]{1,0:T(2,128)S(1)}, f32[2,512]{1,0:T(2,128)S(1)}, f32[2,512]{1,0:T(2,128)S(1)}) fusion(f32[2,512,1024]{2,1,0:T(8,128)} %get-tuple-element.1423, f32[2,512]{1,0:T(2,128)S(1)} %bitcast.403, f32[2,512,1024]{2,1,0:T(8,128)} %get-tuple-element.1424, ...), kind=kLoop, calls=%fused_computation.117.clone.1 | loop fusion | flops 12577792 | bytes 21520384 | tf_op jit(solution)/shard_map/while/body/eval_jaxpr/reduce_sum | solution.py:128
  289.5 4.7 convert_bitcast_fusion.2
  297.0 3.9 fusion.186
  305.0 4.6 fusion.188
  317.0 71.1 %collective-permute-start.8 = (f32[1024,128]{1,0:T(8,128)}, f32[1024,128]{1,0:T(8,128)S(1)}, u32[]{:S(2)}, u32[]{:S(2)}) collective-permute-start(f32[1024,128]{1,0:T(8,128)} %get-tuple-element.666), channel_id=1, source_target_pairs={{4,0},{8,4},{12,8},{16,12},{20,16},{24,20},{28,24},{32,28},{36,32}... | collective-permute-start | bytes 1572872 | tf_op jit(solution)/shard_map/ppermute | solution.py:19
  394.9 3.3 collective-permute-start.14
  398.2 10.4 %collective-permute-done.8 = f32[1024,128]{1,0:T(8,128)S(1)} collective-permute-done((f32[1024,128]{1,0:T(8,128)}, f32[1024,128]{1,0:T(8,128)S(1)}, u32[]{:S(2)}, u32[]{:S(2)}) %collective-permute-start.8) | collective-permute-done | bytes 524320 | tf_op jit(solution)/shard_map/ppermute | solution.py:19
  410.6 9.3 %collective-permute-done.9 = f32[1024,128]{1,0:T(8,128)S(1)} collective-permute-done((f32[1024,128]{1,0:T(8,128)}, f32[1024,128]{1,0:T(8,128)S(1)}, u32[]{:S(2)}, u32[]{:S(2)}) %collective-permute-start.9) | collective-permute-done | bytes 524320 | tf_op jit(solution)/shard_map/ppermute | solution.py:19
  421.0 13.3 %collective-permute-done.12 = f32[1024,128]{1,0:T(8,128)S(1)} collective-permute-done((f32[1024,128]{1,0:T(8,128)}, f32[1024,128]{1,0:T(8,128)S(1)}, u32[]{:S(2)}, u32[]{:S(2)}) %collective-permute-start.12) | collective-permute-done | bytes 524320 | tf_op jit(solution)/shard_map/ppermute | solution.py:19
  434.4 11.2 %collective-permute-done.13 = f32[1024,128]{1,0:T(8,128)S(1)} collective-permute-done((f32[1024,128]{1,0:T(8,128)}, f32[1024,128]{1,0:T(8,128)S(1)}, u32[]{:S(2)}, u32[]{:S(2)}) %collective-permute-start.13) | collective-permute-done | bytes 524320 | tf_op jit(solution)/shard_map/ppermute | solution.py:19
  445.6 11.2 %collective-permute-done.14 = f32[1024,128]{1,0:T(8,128)S(1)} collective-permute-done((f32[1024,128]{1,0:T(8,128)}, f32[1024,128]{1,0:T(8,128)S(1)}, u32[]{:S(2)}, u32[]{:S(2)}) %collective-permute-start.14) | collective-permute-done | bytes 524320 | tf_op jit(solution)/shard_map/ppermute | solution.py:19
  456.9 13.2 %collective-permute-done.15 = f32[1024,128]{1,0:T(8,128)S(1)} collective-permute-done((f32[1024,128]{1,0:T(8,128)}, f32[1024,128]{1,0:T(8,128)S(1)}, u32[]{:S(2)}, u32[]{:S(2)}) %collective-permute-start.15) | collective-permute-done | bytes 524320 | tf_op jit(solution)/shard_map/ppermute | solution.py:19
  472.3 3.9 all-to-all-start
  478.0 14.2 %all-to-all-done = f32[4,256,256]{2,1,0:T(8,128)S(1)} async-done(((f32[4,256,256]{2,1,0:T(8,128)}), f32[4,256,256]{2,1,0:T(8,128)S(1)}, u32[]{:S(2)}, u32[]{:S(2)}) %all-to-all-start) | async-done | bytes 1048608 | tf_op jit(solution)/shard_map/all_to_all | solution.py:30
  (218 shorter events, 126.5 us)
Async XLA Ops:
  0.6 19.3 %collective-permute-start = (bf16[1024,128]{1,0:T(8,128)(2,1)}, bf16[1024,128]{1,0:T(8,128)(2,1)}, u32[]{:S(2)}, u32[]{:S(2)}) collective-permute-start(bf16[1024,128]{1,0:T(8,128)(2,1)} %param.32), channel_id=1, source_target_pairs={{0,4},{4,8},{8,12},{12,16},{16,20},{20,24},{24,28},{28,32},{32,36}... | collective-permute-start | bytes 786440 | tf_op jit(solution)/shard_map/ppermute | solution.py:19
  4.5 17.8 %collective-permute-start.1 = (bf16[1024,128]{1,0:T(8,128)(2,1)}, bf16[1024,128]{1,0:T(8,128)(2,1)}, u32[]{:S(2)}, u32[]{:S(2)}) collective-permute-start(bf16[1024,128]{1,0:T(8,128)(2,1)} %param.32), channel_id=1, source_target_pairs={{0,8},{4,12},{8,16},{12,20},{16,24},{20,28},{24,32},{28,36},{32,40... | collective-permute-start | bytes 786440 | tf_op jit(solution)/shard_map/ppermute | solution.py:19
  10.0 15.9 %collective-permute-start.2 = (bf16[1024,128]{1,0:T(8,128)(2,1)}, bf16[1024,128]{1,0:T(8,128)(2,1)}, u32[]{:S(2)}, u32[]{:S(2)}) collective-permute-start(bf16[1024,128]{1,0:T(8,128)(2,1)} %param.32), channel_id=1, source_target_pairs={{0,12},{4,16},{8,20},{12,24},{16,28},{20,32},{24,36},{28,40},{32,4... | collective-permute-start | bytes 786440 | tf_op jit(solution)/shard_map/ppermute | solution.py:19
  13.4 28.1 %collective-permute-start.3 = (bf16[1024,128]{1,0:T(8,128)(2,1)}, bf16[1024,128]{1,0:T(8,128)(2,1)}, u32[]{:S(2)}, u32[]{:S(2)}) collective-permute-start(bf16[1024,128]{1,0:T(8,128)(2,1)} %param.32), channel_id=1, source_target_pairs={{0,16},{4,20},{8,24},{12,28},{16,32},{20,36},{24,40},{28,44},{32,4... | collective-permute-start | bytes 786440 | tf_op jit(solution)/shard_map/ppermute | solution.py:19
  16.9 24.6 %collective-permute-start.4 = (bf16[1024,128]{1,0:T(8,128)(2,1)}, bf16[1024,128]{1,0:T(8,128)(2,1)}, u32[]{:S(2)}, u32[]{:S(2)}) collective-permute-start(bf16[1024,128]{1,0:T(8,128)(2,1)} %param.33), channel_id=1, source_target_pairs={{0,4},{4,8},{8,12},{12,16},{16,20},{20,24},{24,28},{28,32},{32,36}... | collective-permute-start | bytes 786440 | tf_op jit(solution)/shard_map/ppermute | solution.py:19
  19.9 21.6 %collective-permute-start.5 = (bf16[1024,128]{1,0:T(8,128)(2,1)}, bf16[1024,128]{1,0:T(8,128)(2,1)}, u32[]{:S(2)}, u32[]{:S(2)}) collective-permute-start(bf16[1024,128]{1,0:T(8,128)(2,1)} %param.33), channel_id=1, source_target_pairs={{0,8},{4,12},{8,16},{12,20},{16,24},{20,28},{24,32},{28,36},{32,40... | collective-permute-start | bytes 786440 | tf_op jit(solution)/shard_map/ppermute | solution.py:19
  22.3 19.2 %collective-permute-start.6 = (bf16[1024,128]{1,0:T(8,128)(2,1)}, bf16[1024,128]{1,0:T(8,128)(2,1)}, u32[]{:S(2)}, u32[]{:S(2)}) collective-permute-start(bf16[1024,128]{1,0:T(8,128)(2,1)} %param.33), channel_id=1, source_target_pairs={{0,12},{4,16},{8,20},{12,24},{16,28},{20,32},{24,36},{28,40},{32,4... | collective-permute-start | bytes 786440 | tf_op jit(solution)/shard_map/ppermute | solution.py:19
  25.9 15.6 %collective-permute-start.7 = (bf16[1024,128]{1,0:T(8,128)(2,1)}, bf16[1024,128]{1,0:T(8,128)(2,1)}, u32[]{:S(2)}, u32[]{:S(2)}) collective-permute-start(bf16[1024,128]{1,0:T(8,128)(2,1)} %param.33), channel_id=1, source_target_pairs={{0,16},{4,20},{8,24},{12,28},{16,32},{20,36},{24,40},{28,44},{32,4... | collective-permute-start | bytes 786440 | tf_op jit(solution)/shard_map/ppermute | solution.py:19
  129.6 9.3 %copy-start = (f32[512,2,1024]{2,0,1:T(8,128)}, f32[512,2,1024]{2,0,1:T(8,128)S(1)}, u32[]{:S(2)}) copy-start(f32[512,2,1024]{2,0,1:T(8,128)S(1)} %get-tuple-element.1417) | copy-start | bytes 12582916 | tf_op jit(solution)/shard_map/while
  175.9 4.7 copy-start.9
  203.1 0.9 copy-start.1
  215.2 0.8 copy-start.3
  227.3 0.8 copy-start.5
  228.1 3.9 copy-start.2
  228.1 4.0 copy-start.4
  228.1 4.0 copy-start.6
  232.1 1.8 copy-start.10
  232.1 1.8 copy-start.11
  232.1 1.8 copy-start.14
  234.5 0.8 copy-start.12
  235.3 0.8 copy-start.15
  235.3 5.2 %copy-start.7 = (f32[1024,128]{1,0:T(8,128)S(1)}, f32[1024,128]{1,0:T(8,128)}, u32[]{:S(2)}) copy-start(f32[1024,128]{1,0:T(8,128)} %get-tuple-element.1558) | copy-start | bytes 1572868 | tf_op jit(solution)/shard_map/while
  241.4 0.8 copy-start.8
  276.6 9.3 %copy-start = (f32[512,2,1024]{2,0,1:T(8,128)}, f32[512,2,1024]{2,0,1:T(8,128)S(1)}, u32[]{:S(2)}) copy-start(f32[512,2,1024]{2,0,1:T(8,128)S(1)} %get-tuple-element.1417) | copy-start | bytes 12582916 | tf_op jit(solution)/shard_map/while
  289.5 4.7 copy-start.9
  294.4 0.9 copy-start.1
  295.3 0.8 copy-start.3
  296.2 0.8 copy-start.5
  297.0 3.9 copy-start.2
  297.0 4.0 copy-start.4
  297.0 4.0 copy-start.6
  300.9 1.8 copy-start.10
  301.0 1.8 copy-start.11
  301.0 1.8 copy-start.14
  303.4 0.8 copy-start.12
  304.2 0.8 copy-start.15
  304.2 5.4 %copy-start.7 = (f32[1024,128]{1,0:T(8,128)S(1)}, f32[1024,128]{1,0:T(8,128)}, u32[]{:S(2)}) copy-start(f32[1024,128]{1,0:T(8,128)} %get-tuple-element.1558) | copy-start | bytes 1572868 | tf_op jit(solution)/shard_map/while
  310.5 0.8 copy-start.8
  313.1 79.0 %collective-permute-start.10 = (f32[1024,128]{1,0:T(8,128)}, f32[1024,128]{1,0:T(8,128)S(1)}, u32[]{:S(2)}, u32[]{:S(2)}) collective-permute-start(f32[1024,128]{1,0:T(8,128)} %get-tuple-element.668), channel_id=1, source_target_pairs={{12,0},{16,4},{20,8},{24,12},{28,16},{32,20},{36,24},{40,28},{44,3... | collective-permute-start | bytes 1572872 | tf_op jit(solution)/shard_map/ppermute | solution.py:19
  315.1 79.9 %collective-permute-start.11 = (f32[1024,128]{1,0:T(8,128)}, f32[1024,128]{1,0:T(8,128)S(1)}, u32[]{:S(2)}, u32[]{:S(2)}) collective-permute-start(f32[1024,128]{1,0:T(8,128)} %get-tuple-element.669), channel_id=1, source_target_pairs={{16,0},{20,4},{24,8},{28,12},{32,16},{36,20},{40,24},{44,28},{48,3... | collective-permute-start | bytes 1572872 | tf_op jit(solution)/shard_map/ppermute | solution.py:19
  317.0 91.7 %collective-permute-start.8 = (f32[1024,128]{1,0:T(8,128)}, f32[1024,128]{1,0:T(8,128)S(1)}, u32[]{:S(2)}, u32[]{:S(2)}) collective-permute-start(f32[1024,128]{1,0:T(8,128)} %get-tuple-element.666), channel_id=1, source_target_pairs={{4,0},{8,4},{12,8},{16,12},{20,16},{24,20},{28,24},{32,28},{36,32}... | collective-permute-start | bytes 1572872 | tf_op jit(solution)/shard_map/ppermute | solution.py:19
  388.1 31.7 %collective-permute-start.9 = (f32[1024,128]{1,0:T(8,128)}, f32[1024,128]{1,0:T(8,128)S(1)}, u32[]{:S(2)}, u32[]{:S(2)}) collective-permute-start(f32[1024,128]{1,0:T(8,128)} %get-tuple-element.667), channel_id=1, source_target_pairs={{8,0},{12,4},{16,8},{20,12},{24,16},{28,20},{32,24},{36,28},{40,32... | collective-permute-start | bytes 1572872 | tf_op jit(solution)/shard_map/ppermute | solution.py:19
  390.1 44.3 %collective-permute-start.12 = (f32[1024,128]{1,0:T(8,128)}, f32[1024,128]{1,0:T(8,128)S(1)}, u32[]{:S(2)}, u32[]{:S(2)}) collective-permute-start(f32[1024,128]{1,0:T(8,128)} %get-tuple-element.671), channel_id=1, source_target_pairs={{4,0},{8,4},{12,8},{16,12},{20,16},{24,20},{28,24},{32,28},{36,32}... | collective-permute-start | bytes 1572872 | tf_op jit(solution)/shard_map/ppermute | solution.py:19
  392.2 53.5 %collective-permute-start.13 = (f32[1024,128]{1,0:T(8,128)}, f32[1024,128]{1,0:T(8,128)S(1)}, u32[]{:S(2)}, u32[]{:S(2)}) collective-permute-start(f32[1024,128]{1,0:T(8,128)} %get-tuple-element.672), channel_id=1, source_target_pairs={{8,0},{12,4},{16,8},{20,12},{24,16},{28,20},{32,24},{36,28},{40,32... | collective-permute-start | bytes 1572872 | tf_op jit(solution)/shard_map/ppermute | solution.py:19
  394.9 61.9 %collective-permute-start.14 = (f32[1024,128]{1,0:T(8,128)}, f32[1024,128]{1,0:T(8,128)S(1)}, u32[]{:S(2)}, u32[]{:S(2)}) collective-permute-start(f32[1024,128]{1,0:T(8,128)} %get-tuple-element.673), channel_id=1, source_target_pairs={{12,0},{16,4},{20,8},{24,12},{28,16},{32,20},{36,24},{40,28},{44,3... | collective-permute-start | bytes 1572872 | tf_op jit(solution)/shard_map/ppermute | solution.py:19
  408.6 61.4 %collective-permute-start.15 = (f32[1024,128]{1,0:T(8,128)}, f32[1024,128]{1,0:T(8,128)S(1)}, u32[]{:S(2)}, u32[]{:S(2)}) collective-permute-start(f32[1024,128]{1,0:T(8,128)} %get-tuple-element.674), channel_id=1, source_target_pairs={{16,0},{20,4},{24,8},{28,12},{32,16},{36,20},{40,24},{44,28},{48,3... | collective-permute-start | bytes 1572872 | tf_op jit(solution)/shard_map/ppermute | solution.py:19
  421.0 55.2 %copy-start.16 = (bf16[2,512,2,128]{3,2,1,0:T(2,128)(2,1)S(1)}, bf16[2,512,2,128]{3,2,1,0:T(2,128)(2,1)}, u32[]{:S(2)}) copy-start(bf16[2,512,2,128]{3,2,1,0:T(2,128)(2,1)} %get-tuple-element.664) | copy-start | bytes 1572868
  470.0 7.1 %copy-start.13 = (bf16[2,512,2,128]{3,2,1,0:T(2,128)(2,1)S(1)}, bf16[2,512,2,128]{3,2,1,0:T(2,128)(2,1)}, u32[]{:S(2)}) copy-start(bf16[2,512,2,128]{3,2,1,0:T(2,128)(2,1)} %get-tuple-element.663) | copy-start | bytes 1572868
  472.3 19.9 %all-to-all-start = ((f32[4,256,256]{2,1,0:T(8,128)}), f32[4,256,256]{2,1,0:T(8,128)S(1)}, u32[]{:S(2)}, u32[]{:S(2)}) async-start(f32[4,256,256]{2,1,0:T(8,128)} %bitcast.49), calls=%async_computation | async-start | bytes 2097152 | tf_op jit(solution)/shard_map/all_to_all | solution.py:30
where the time goes:
time: 498 us; the launch traced here: 493 us
  starting transfers between devices  118 us (24%)
  matrix products  112 us (22%)
  local copies, waits for them, and re-layouts  110 us (22%)
  waiting for transfers between devices  82.9 us (17%)
  loops' own time  36.8 us (7%)
  other arithmetic  29.9 us (6%)
    ppermute x16, starting transfers between devices, passed_along(): return lax.ppermute(x, axis, pairs)  114 us
    ppermute x16, waiting for transfers between devices, passed_along(): return lax.ppermute(x, axis, pairs)  68.7 us
    another operation x29, local copies, waits for them, and re-layouts  51 us
    another operation x1, loops' own time, attend(): lax.scan(per_block, start_state, blocks)  36.4 us
    dot_general x6, matrix products, backward_piece(): jnp.einsum('hqk,qhd->kd', probs_low, grad_block, preferred_element_type=j...  24.4 us
    dot_general x6, matrix products, forward_piece(): jnp.einsum('hqk,kd->qhd', probs_low, vmatrix, preferred_element_type=jnp....  22.8 us
    dot_general x6, matrix products, block_scores(): jnp.einsum('qhd,kd->hqk', query_block, kmatrix, preferred_element_type=jn...  21.9 us
    cond x4, local copies, waits for them, and re-layouts, guarded(): return lax.cond(needed, compute, blank_fn)  21.6 us
  transfers between devices with their start and end apart: 17, of which 7 were waited for; matrix products, arithmetic and copies ran while one was open for 3% of the time, Pallas kernels for 0%

commit v1 on v0

v1 whole, which is shorter than its diff:
```python
import math

import jax
import jax.numpy as jnp
from jax import lax
from jax.experimental import pallas as pl
from jax.experimental.pallas import tpu as pltpu
from jax.sharding import PartitionSpec as P

DH = 128
SPAN = 4
ROWS = 1024
WIN = (SPAN + 1) * ROWS
HL = 2
BQ = 512
BK = 512
M = HL * BQ
QUARTER = ROWS // 4
masked_score = -1e30
F32 = jnp.float32
BF16 = jnp.bfloat16
ROW_ROW = (((1,), (1,)), ((), ()))
ROW_COL = (((1,), (0,)), ((), ()))


def dot(a, b, dims):
    return lax.dot_general(a, b, dims, preferred_element_type=F32)


def attn_kernel(sc_ref, begin_ref, q_ref, g_ref, k_hbm, v_hbm, *rest):
    mine = rest[:SPAN]
    other = rest[SPAN : 2 * SPAN]
    o_ref, dq_ref, send_ref, keep_ref = rest[2 * SPAN : 2 * SPAN + 4]
    kv, kt, vt, s_scr, dk, dv, ot_s, dq_s, g_s, q_s, stage, sem, out_sem = rest[2 * SPAN + 4 :]
    nq = ROWS // BQ
    core = sc_ref[2 * nq]
    kw = kv.at[0]
    vw = kv.at[1]
    copies = []
    for src, side, d in (
        [(k_hbm, 0, 0), (v_hbm, 1, 0)]
        + [(mine[d - 1], core, d) for d in range(1, SPAN + 1)]
        + [(other[d - 1], 1 - core, d) for d in range(1, SPAN + 1)]
    ):
        dst = kv.at[side, pl.ds((SPAN - d) * ROWS, ROWS), :]
        copies.append(pltpu.make_async_copy(src, dst, sem.at[len(copies)]))
    for c in copies:
        c.start()
    dk[...] = jnp.zeros_like(dk)
    dv[...] = jnp.zeros_like(dv)
    for c in copies:
        c.wait()

    def krow(j):
        return pl.ds(pl.multiple_of(j * BK, BK), BK)

    @pl.loop(sc_ref[0] // BK, WIN // BK)
    def _(j):
        kt[:, krow(j)] = kw[krow(j), :].T
        vt[:, krow(j)] = vw[krow(j), :].T

    fac = 1.0 / math.sqrt(DH)
    c2 = math.log2(math.e) * fac

    @pl.loop(0, nq)
    def _(qb):
        qr = pl.ds(pl.multiple_of(qb * BQ, BQ), BQ)
        for h in range(HL):
            q_s[h * BQ : (h + 1) * BQ, :] = q_ref[qr, h * DH : (h + 1) * DH]
        diag = (SPAN * ROWS) // BK + qb
        lo = sc_ref[qb] // BK
        full = jnp.minimum((sc_ref[nq + qb] + BK - 1) // BK, diag)
        beg = jnp.concatenate([begin_ref[:, qr]] * HL, axis=1)

        def score(j, m, masked):
            s = dot(kw[krow(j), :], q_s[...], ROW_ROW)
            if masked:
                kp = j * BK + lax.broadcasted_iota(jnp.int32, (BK, M), 0)
                qp = diag * BK + (lax.broadcasted_iota(jnp.int32, (1, M), 1) & (BQ - 1))
                s = jnp.where((kp >= beg) & (kp <= qp), s, masked_score)
            s_scr[krow(j), :] = s
            return jnp.maximum(m, jnp.max(s.reshape(BK // 8, 8, M), axis=0))

        def masked_body(i, m):
            return score(jnp.where(i == 0, diag, lo + i - 1), m, True)

        m = jnp.full((8, M), masked_score, F32)
        m = lax.fori_loop(0, 1 + full - lo, masked_body, m)
        m = lax.fori_loop(full, diag, lambda j, m: score(j, m, False), m)
        top = jnp.max(m, axis=0, keepdims=True) * c2
        ot_s[...] = jnp.zeros_like(ot_s)
        dq_s[...] = jnp.zeros_like(dq_s)

        def forward_body(j, total):
            p = jnp.exp2(s_scr[krow(j), :] * c2 - top)
            s_scr[krow(j), :] = p
            ot_s[...] += dot(vt[:, krow(j)], p.astype(BF16), ROW_COL)
            return total + jnp.sum(p.reshape(BK // 8, 8, M), axis=0)

        total = lax.fori_loop(lo, diag + 1, forward_body, jnp.zeros((8, M), F32))
        inv = 1.0 / jnp.sum(total, axis=0, keepdims=True)
        out_t = ot_s[...] * inv
        g_t = jnp.concatenate([g_ref[qr, h * DH : (h + 1) * DH].T for h in range(HL)], axis=1)
        g_t = (g_t.astype(F32) * inv).astype(BF16)
        g_s[...] = g_t.T
        out_low = out_t.astype(BF16)
        for h in range(HL):
            o_ref[qr, h * DH : (h + 1) * DH] = out_low[:, h * BQ : (h + 1) * BQ].T
        delta = jnp.sum(g_t.astype(F32) * out_t, axis=0, keepdims=True)

        def backward_body(j, carry):
            kr = krow(j)
            dp = dot(vw[kr, :], g_s[...], ROW_ROW)
            p = s_scr[kr, :]
            ds = (p * (dp - delta)).astype(BF16)
            dq_s[...] += dot(kt[:, kr], ds, ROW_COL)
            dk[kr, :] += dot(ds, q_s[...], ROW_COL)
            dv[kr, :] += dot(p.astype(BF16), g_s[...], ROW_COL)
            return carry

        lax.fori_loop(lo, diag + 1, backward_body, 0)
        dq_low = (dq_s[...] * fac).astype(BF16)
        for h in range(HL):
            dq_ref[qr, h * DH : (h + 1) * DH] = dq_low[:, h * BQ : (h + 1) * BQ].T

    outs = []
    for side, dst in ((1 - core, send_ref), (core, keep_ref)):
        for w in range(SPAN + 1):
            slot = len(outs)
            for t in range(2):
                start = pl.multiple_of(w * ROWS + (2 * t + side) * QUARTER, QUARTER)
                rows = pl.ds(start, QUARTER)
                stage[slot, t, :, 0:DH] = (dk[rows, :] * fac).astype(BF16)
                stage[slot, t, :, DH : 2 * DH] = dv[rows, :].astype(BF16)
            outs.append(pltpu.make_async_copy(stage.at[slot], dst.at[w], out_sem.at[slot]))
            outs[-1].start()
    for c in outs:
        c.wait()


def attention(scalars, begin, q, g, k, v, mine, other):
    anywhere = pl.BlockSpec(memory_space=pl.ANY)
    vmem = pl.BlockSpec(memory_space=pltpu.VMEM)
    part = (SPAN + 1, 2, QUARTER, 2 * DH)
    return pl.pallas_call(
        attn_kernel,
        out_shape=(
            jax.ShapeDtypeStruct((ROWS, HL * DH), BF16),
            jax.ShapeDtypeStruct((ROWS, HL * DH), BF16),
            jax.ShapeDtypeStruct(part, BF16),
            jax.ShapeDtypeStruct(part, BF16),
        ),
        in_specs=[pl.BlockSpec(memory_space=pltpu.SMEM), vmem, vmem, vmem]
        + [anywhere] * (2 + 2 * SPAN),
        out_specs=(vmem, vmem, anywhere, anywhere),
        scratch_shapes=[
            pltpu.VMEM((2, WIN, DH), BF16),
            pltpu.VMEM((DH, WIN), BF16),
            pltpu.VMEM((DH, WIN), BF16),
            pltpu.VMEM((WIN, M), F32),
            pltpu.VMEM((WIN, DH), F32),
            pltpu.VMEM((WIN, DH), F32),
            pltpu.VMEM((DH, M), F32),
            pltpu.VMEM((DH, M), F32),
            pltpu.VMEM((M, DH), BF16),
            pltpu.VMEM((M, DH), BF16),
            pltpu.VMEM((2 * (SPAN + 1), 2, QUARTER, 2 * DH), BF16),
            pltpu.SemaphoreType.DMA((2 + 2 * SPAN,)),
            pltpu.SemaphoreType.DMA((2 * (SPAN + 1),)),
        ],
        compiler_params=pltpu.CompilerParams(vmem_limit_bytes=60 * 2**20),
        name="attn",
    )(scalars, begin, q, g, k, v, *mine, *other)


def along_ctx(x, by):
    count = lax.axis_size("ctx")
    return lax.ppermute(x, "ctx", [(i, (i + by) % count) for i in range(count)])


def along_head(x, flip):
    return lax.ppermute(x, "head", [(i, i ^ flip) for i in range(4)])


def shards(queries, keys, values, grad_out, lengths):
    place = lax.axis_index("ctx")
    head = lax.axis_index("head")
    core = head % 2
    side = head // 2
    carried = jnp.where(core == 0, keys, values)
    mine = [along_ctx(carried, d) for d in range(1, SPAN + 1)]
    other = [along_head(x, 1) for x in mine]

    docs = jnp.arange(lengths.shape[0])
    ends = jnp.sum(jnp.where(docs[None, :] <= docs[:, None], lengths[None, :], 0), axis=1)
    own = place * ROWS + jnp.arange(ROWS, dtype=jnp.int32)
    begin = jnp.max(jnp.where(ends[:, None] <= own[None, :], ends[:, None], 0), axis=0)
    begin = begin - (place - SPAN) * ROWS
    scalars = jnp.concatenate([begin[::BQ], begin[BQ - 1 :: BQ], core[None]]).astype(jnp.int32)

    out, grad_q, send, keep = attention(
        scalars, begin.reshape(1, ROWS), queries, grad_out, keys, values, mine, other
    )
    swapped = along_head(send, 1)
    totals = [
        keep[SPAN - d].astype(F32) + swapped[SPAN - d].astype(F32) for d in range(SPAN + 1)
    ]
    acc = totals[0]
    for d in range(1, SPAN + 1):
        acc = acc + along_ctx(totals[d].astype(BF16), -d).astype(F32)
    give = lax.dynamic_index_in_dim(acc, 1 - side, 0, keepdims=False).astype(BF16)
    stay = lax.dynamic_index_in_dim(acc, side, 0, keepdims=False)
    done = (stay + along_head(give, 2).astype(F32)).astype(BF16)
    return out, grad_q, done[:, :DH], done[:, DH:]


def solution(mesh):
    placed = (P("ctx", "head"), P("ctx", None), P("ctx", None), P("ctx", "head"), P())
    return jax.shard_map(
        shards,
        mesh=mesh,
        in_specs=placed,
        out_specs=(
            P("ctx", "head"),
            P("ctx", "head"),
            P(("ctx", "head"), None),
            P(("ctx", "head"), None),
        ),
        check_vma=False,
    )
```

time: 498 us -> 117 us (0.23)
  matrix products: 112 us -> 0 us
  local copies, waits for them, and re-layouts: 110 us -> 1.54 us
  starting transfers between devices: 118 us -> 36.6 us
  loops' own time: 36.8 us -> 0 us
  waiting for transfers between devices: 82.9 us -> 54.7 us
  other arithmetic: 29.9 us -> 5.09 us
  Pallas kernels: 0 us -> 18.1 us
    dot_general x36 -> x0, matrix products: 112 us -> none  [the longest x6 24.4 us: backward_piece(): jnp.einsum('hqk,qhd->kd', probs_low, grad_block, preferred_element_type=j...]
    ppermute x16 -> x14, starting transfers between devices: 114 us -> 36.6 us  [the longest x8 33.9 us: along_ctx(): return lax.ppermute(x, 'ctx', [(i, (i + by) % count) for i in range(count)])]
    another operation x29 -> x0, local copies, waits for them, and re-layouts: 51 us -> none
    another operation x25 -> x0, loops' own time: 36.8 us -> none  [the longest x1 36.4 us: attend(): lax.scan(per_block, start_state, blocks)]
    cond x8 -> x0, local copies, waits for them, and re-layouts: 24.3 us -> none  [the longest x4 21.6 us: guarded(): return lax.cond(needed, compute, blank_fn)]
    reduce_sum x4 -> x1, other arithmetic: 20.3 us -> 0.76 us  [shards(): jnp.sum(jnp.where(docs[None, :] <= docs[:, None], lengths[None, :], 0), a...]
    pallas_call x0 -> x1, Pallas kernels: none -> 18.1 us  [attention(): pl.pallas_call(attn_kernel, out_shape=(jax.ShapeDtypeStruct((ROWS, HL * D...]
    all_to_all x1 -> x0, waiting for transfers between devices: 14.2 us -> none  [sent_and_summed(): lax.all_to_all(tiles, axis, split_axis=0, concat_axis=0, tiled=True)]
  transfers between devices with their start and end apart: 17 -> 14, of which waited for: 7 -> 10; matrix products, arithmetic and copies ran while one was open for 3% -> 1% of each run, Pallas kernels for 0% -> 0%
where the time goes in v1:
time: 117 us
  waiting for transfers between devices  54.7 us (47%)
  starting transfers between devices  36.6 us (31%)
  Pallas kernels  18.1 us (15%)
  other arithmetic  5.09 us (4%)
  local copies, waits for them, and re-layouts  1.54 us (1%)
    ppermute x8, waiting for transfers between devices, along_ctx(): return lax.ppermute(x, 'ctx', [(i, (i + by) % count) for i in range(count)])  46.6 us
    ppermute x8, starting transfers between devices, along_ctx(): return lax.ppermute(x, 'ctx', [(i, (i + by) % count) for i in range(count)])  33.9 us
    pallas_call x1, Pallas kernels, attention(): pl.pallas_call(attn_kernel, out_shape=(jax.ShapeDtypeStruct((ROWS, HL * D...  18.1 us
    ppermute x6, waiting for transfers between devices, along_head(): return lax.ppermute(x, 'head', [(i, i ^ flip) for i in range(4)])  8.03 us
    ppermute x6, starting transfers between devices, along_head(): return lax.ppermute(x, 'head', [(i, i ^ flip) for i in range(4)])  2.68 us
  transfers between devices with their start and end apart: 14, of which 10 were waited for; matrix products, arithmetic and copies ran while one was open for 1% of the time, Pallas kernels for 0%

profile of v1, /device:TPU:12, one launch (start us, length us, event | category | flops | bytes accessed | tf_op | source)
XLA Modules:
  0.0 116.8 jit_solution(286489117317402808)
XLA Ops:
  0.6 1.0 broadcast_select_fusion
  1.6 1.2 collective-permute-start.3
  2.8 4.0 %collective-permute-start.2 = (bf16[1024,128]{1,0:T(8,128)(2,1)S(1)}, bf16[1024,128]{1,0:T(8,128)(2,1)S(1)}, u32[]{:S(2)}, u32[]{:S(2)}) collective-permute-start(bf16[1024,128]{1,0:T(8,128)(2,1)S(1)} %broadcast_select_fusion), channel_id=1, source_target_pairs={{0,12},{4,16},{8,20},{12,24},{16,28},{20,32},{24,36},{28,40},{32,4... | collective-permute-start | bytes 786440 | tf_op jit(solution)/shard_map/ppermute | solution.py:178
  6.8 1.0 collective-permute-start.1
  7.8 1.3 %collective-permute-start = (bf16[1024,128]{1,0:T(8,128)(2,1)S(1)}, bf16[1024,128]{1,0:T(8,128)(2,1)S(1)}, u32[]{:S(2)}, u32[]{:S(2)}) collective-permute-start(bf16[1024,128]{1,0:T(8,128)(2,1)S(1)} %broadcast_select_fusion), channel_id=1, source_target_pairs={{0,4},{4,8},{8,12},{12,16},{16,20},{20,24},{24,28},{28,32},{32,36}... | collective-permute-start | bytes 786440 | tf_op jit(solution)/shard_map/ppermute | solution.py:178
  9.1 0.8 select_reduce_fusion.1
  9.9 0.2 select_reduce_fusion
  10.0 0.0 collective-permute-done.3.rest_3_
  10.0 0.0 copy-start
  10.1 0.1 collective-permute-start.7
  10.1 6.7 %collective-permute-done.2.rest_2_ = bf16[1024,128]{1,0:T(8,128)(2,1)S(1)} collective-permute-done((bf16[1024,128]{1,0:T(8,128)(2,1)S(1)}, bf16[1024,128]{1,0:T(8,128)(2,1)S(1)}, u32[]{:S(2)}, u32[]{:S(2)}) %collective-permute-start.2) | collective-permute-done | bytes 262176 | tf_op jit(solution)/shard_map/ppermute | solution.py:178
  16.8 0.0 copy-start.1
  16.8 0.0 collective-permute-start.6
  16.8 8.0 %collective-permute-done.1.rest_1_ = bf16[1024,128]{1,0:T(8,128)(2,1)S(1)} collective-permute-done((bf16[1024,128]{1,0:T(8,128)(2,1)S(1)}, bf16[1024,128]{1,0:T(8,128)(2,1)S(1)}, u32[]{:S(2)}, u32[]{:S(2)}) %collective-permute-start.1) | collective-permute-done | bytes 262176 | tf_op jit(solution)/shard_map/ppermute | solution.py:178
  24.8 0.0 copy-start.2
  24.8 0.0 collective-permute-start.5
  24.8 5.3 %collective-permute-done.rest_0_ = bf16[1024,128]{1,0:T(8,128)(2,1)S(1)} collective-permute-done((bf16[1024,128]{1,0:T(8,128)(2,1)S(1)}, bf16[1024,128]{1,0:T(8,128)(2,1)S(1)}, u32[]{:S(2)}, u32[]{:S(2)}) %collective-permute-start) | collective-permute-done | bytes 262176 | tf_op jit(solution)/shard_map/ppermute | solution.py:178
  30.1 0.0 copy-start.3
  30.1 0.0 collective-permute-start.4
  30.1 0.0 copy-start.8
  30.1 0.1 slice.43
  30.2 0.1 slice.42
  30.3 0.6 pad_add_fusion.sc_ref
  30.8 0.0 collective-permute-done.7.rest_7_
  30.8 0.0 copy-start.4
  30.8 0.0 collective-permute-done.6.rest_6_
  30.9 0.0 copy-start.5
  30.9 0.0 collective-permute-done.5.rest_5_
  30.9 0.0 copy-start.6
  30.9 0.7 collective-permute-done.4.rest_4_
  31.6 0.0 copy-start.7
  31.6 0.0 copy-done
  31.6 0.0 copy-done.1
  31.6 0.0 copy-done.2
  31.6 0.0 copy-done.3
  31.6 0.0 copy-done.8
  31.7 0.0 copy-done.4
  31.7 0.0 copy-done.5
  31.7 0.1 copy-done.6
  31.8 0.6 copy-done.7
  32.3 18.1 %attn.1 = (bf16[1024,256]{1,0:T(8,128)(2,1)}, bf16[1024,256]{1,0:T(8,128)(2,1)}, bf16[5,2,256,256]{3,2,1,0:T(8,128)(2,1)}, bf16[5,2,256,256]{3,2,1,0:T(8,128)(2,1)}) custom-call(s32[5]{0:T(128)} %pad_add_fusion.sc_ref, s32[1,1024]{1,0:T(1,128)} %bitcast.24, bf16[1024,256]{1,0:T(8,128)(2,1)} %q_ref.1, bf16[1024,256]{1,0:T(8,128)(2,1)} %g_ref.1, ...), custom_call_target="tpu_custom_call" | custom-call | tf_op jit(solution)/shard_map/attn/pallas_call | solution.py:145
  50.4 0.2 collective-permute-start.8
  50.6 3.1 %collective-permute-done.8 = bf16[5,2,256,256]{3,2,1,0:T(8,128)(2,1)S(1)} collective-permute-done((bf16[5,2,256,256]{3,2,1,0:T(8,128)(2,1)}, bf16[5,2,256,256]{3,2,1,0:T(8,128)(2,1)S(1)}, u32[]{:S(2)}, u32[]{:S(2)}) %collective-permute-start.8) | collective-permute-done | bytes 1310752 | tf_op jit(solution)/shard_map/ppermute | solution.py:182
  53.7 1.4 %fusion.3 = (bf16[2,256,256]{2,1,0:T(8,128)(2,1)S(1)}, bf16[2,256,256]{2,1,0:T(8,128)(2,1)S(1)}, bf16[2,256,256]{2,1,0:T(8,128)(2,1)S(1)}, bf16[2,256,256]{2,1,0:T(8,128)(2,1)S(1)}) fusion(bf16[5,2,256,256]{3,2,1,0:T(8,128)(2,1)S(1)} %collective-permute-done.8, bf16[5,2,256,256]{3,2,1,0:T(8,128)(2,1)} %get-tuple-element.10), kind=kLoop, calls=%fused_computation.9 | loop fusion | flops 2097152 | bytes 3145728 | tf_op jit(solution)/shard_map/convert_element_type | solution.py:210
  55.2 26.5 %collective-permute-start.9 = (bf16[2,256,256]{2,1,0:T(8,128)(2,1)S(1)}, bf16[2,256,256]{2,1,0:T(8,128)(2,1)S(1)}, u32[]{:S(2)}, u32[]{:S(2)}) collective-permute-start(bf16[2,256,256]{2,1,0:T(8,128)(2,1)S(1)} %get-tuple-element.12), channel_id=1, source_target_pairs={{0,124},{4,0},{8,4},{12,8},{16,12},{20,16},{24,20},{28,24},{32,28}... | collective-permute-start | bytes 786440 | tf_op jit(solution)/shard_map/ppermute | solution.py:178
  81.6 0.0 collective-permute-start.12
  81.6 0.0 collective-permute-start.11
  81.6 0.0 collective-permute-start.10
  81.7 10.7 %collective-permute-done.9 = bf16[2,256,256]{2,1,0:T(8,128)(2,1)S(1)} collective-permute-done((bf16[2,256,256]{2,1,0:T(8,128)(2,1)S(1)}, bf16[2,256,256]{2,1,0:T(8,128)(2,1)S(1)}, u32[]{:S(2)}, u32[]{:S(2)}) %collective-permute-start.9) | collective-permute-done | bytes 262176 | tf_op jit(solution)/shard_map/ppermute | solution.py:178
  92.4 5.6 %collective-permute-done.12 = bf16[2,256,256]{2,1,0:T(8,128)(2,1)S(1)} collective-permute-done((bf16[2,256,256]{2,1,0:T(8,128)(2,1)S(1)}, bf16[2,256,256]{2,1,0:T(8,128)(2,1)S(1)}, u32[]{:S(2)}, u32[]{:S(2)}) %collective-permute-start.12) | collective-permute-done | bytes 262176 | tf_op jit(solution)/shard_map/ppermute | solution.py:178
  98.0 5.6 %collective-permute-done.11 = bf16[2,256,256]{2,1,0:T(8,128)(2,1)S(1)} collective-permute-done((bf16[2,256,256]{2,1,0:T(8,128)(2,1)S(1)}, bf16[2,256,256]{2,1,0:T(8,128)(2,1)S(1)}, u32[]{:S(2)}, u32[]{:S(2)}) %collective-permute-start.11) | collective-permute-done | bytes 262176 | tf_op jit(solution)/shard_map/ppermute | solution.py:178
  103.6 4.8 %collective-permute-done.10 = bf16[2,256,256]{2,1,0:T(8,128)(2,1)S(1)} collective-permute-done((bf16[2,256,256]{2,1,0:T(8,128)(2,1)S(1)}, bf16[2,256,256]{2,1,0:T(8,128)(2,1)S(1)}, u32[]{:S(2)}, u32[]{:S(2)}) %collective-permute-start.10) | collective-permute-done | bytes 262176 | tf_op jit(solution)/shard_map/ppermute | solution.py:178
  108.4 1.1 fusion.2
  109.6 2.4 %collective-permute-start.13 = (bf16[256,256]{1,0:T(8,128)(2,1)S(1)}, bf16[256,256]{1,0:T(8,128)(2,1)S(1)}, u32[]{:S(2)}, u32[]{:S(2)}) collective-permute-start(bf16[256,256]{1,0:T(8,128)(2,1)S(1)} %fusion.8), channel_id=1, source_target_pairs={{0,2},{1,3},{2,0},{3,1},{4,6},{5,7},{6,4},{7,5},{8,10},{9,11},{10,... | collective-permute-start | bytes 393224 | tf_op jit(solution)/shard_map/ppermute | solution.py:182
  111.9 4.2 %collective-permute-done.13 = bf16[256,256]{1,0:T(8,128)(2,1)S(1)} collective-permute-done((bf16[256,256]{1,0:T(8,128)(2,1)S(1)}, bf16[256,256]{1,0:T(8,128)(2,1)S(1)}, u32[]{:S(2)}, u32[]{:S(2)}) %collective-permute-start.13) | collective-permute-done | bytes 131104 | tf_op jit(solution)/shard_map/ppermute | solution.py:182
  116.1 0.7 fusion.9
  (4 shorter events, 0.1 us)
Async XLA Ops:
  1.6 8.4 %collective-permute-start.3 = (bf16[1024,128]{1,0:T(8,128)(2,1)S(1)}, bf16[1024,128]{1,0:T(8,128)(2,1)S(1)}, u32[]{:S(2)}, u32[]{:S(2)}) collective-permute-start(bf16[1024,128]{1,0:T(8,128)(2,1)S(1)} %broadcast_select_fusion), channel_id=1, source_target_pairs={{0,16},{4,20},{8,24},{12,28},{16,32},{20,36},{24,40},{28,44},{32,4... | collective-permute-start | bytes 786440 | tf_op jit(solution)/shard_map/ppermute | solution.py:178
  2.8 14.0 %collective-permute-start.2 = (bf16[1024,128]{1,0:T(8,128)(2,1)S(1)}, bf16[1024,128]{1,0:T(8,128)(2,1)S(1)}, u32[]{:S(2)}, u32[]{:S(2)}) collective-permute-start(bf16[1024,128]{1,0:T(8,128)(2,1)S(1)} %broadcast_select_fusion), channel_id=1, source_target_pairs={{0,12},{4,16},{8,20},{12,24},{16,28},{20,32},{24,36},{28,40},{32,4... | collective-permute-start | bytes 786440 | tf_op jit(solution)/shard_map/ppermute | solution.py:178
  6.8 18.0 %collective-permute-start.1 = (bf16[1024,128]{1,0:T(8,128)(2,1)S(1)}, bf16[1024,128]{1,0:T(8,128)(2,1)S(1)}, u32[]{:S(2)}, u32[]{:S(2)}) collective-permute-start(bf16[1024,128]{1,0:T(8,128)(2,1)S(1)} %broadcast_select_fusion), channel_id=1, source_target_pairs={{0,8},{4,12},{8,16},{12,20},{16,24},{20,28},{24,32},{28,36},{32,40... | collective-permute-start | bytes 786440 | tf_op jit(solution)/shard_map/ppermute | solution.py:178
  7.8 22.3 %collective-permute-start = (bf16[1024,128]{1,0:T(8,128)(2,1)S(1)}, bf16[1024,128]{1,0:T(8,128)(2,1)S(1)}, u32[]{:S(2)}, u32[]{:S(2)}) collective-permute-start(bf16[1024,128]{1,0:T(8,128)(2,1)S(1)} %broadcast_select_fusion), channel_id=1, source_target_pairs={{0,4},{4,8},{8,12},{12,16},{16,20},{20,24},{24,28},{28,32},{32,36}... | collective-permute-start | bytes 786440 | tf_op jit(solution)/shard_map/ppermute | solution.py:178
  10.0 21.6 %copy-start = (bf16[1024,128]{1,0:T(8,128)(2,1)}, bf16[1024,128]{1,0:T(8,128)(2,1)S(1)}, u32[]{:S(2)}) copy-start(bf16[1024,128]{1,0:T(8,128)(2,1)S(1)} %collective-permute-done.3.rest_3_) | copy-start | bytes 786436
  10.1 20.8 %collective-permute-start.7 = (bf16[1024,128]{1,0:T(8,128)(2,1)S(1)}, bf16[1024,128]{1,0:T(8,128)(2,1)S(1)}, u32[]{:S(2)}, u32[]{:S(2)}) collective-permute-start(bf16[1024,128]{1,0:T(8,128)(2,1)S(1)} %collective-permute-done.3.rest_3_), channel_id=1, source_target_pairs={{0,1},{1,0},{2,3},{3,2},{4,5},{5,4},{6,7},{7,6},{8,9},{9,8},{10,11... | collective-permute-start | bytes 786440 | tf_op jit(solution)/shard_map/ppermute | solution.py:182
  16.8 14.8 %copy-start.1 = (bf16[1024,128]{1,0:T(8,128)(2,1)}, bf16[1024,128]{1,0:T(8,128)(2,1)S(1)}, u32[]{:S(2)}) copy-start(bf16[1024,128]{1,0:T(8,128)(2,1)S(1)} %collective-permute-done.2.rest_2_) | copy-start | bytes 786436
  16.8 14.0 %collective-permute-start.6 = (bf16[1024,128]{1,0:T(8,128)(2,1)S(1)}, bf16[1024,128]{1,0:T(8,128)(2,1)S(1)}, u32[]{:S(2)}, u32[]{:S(2)}) collective-permute-start(bf16[1024,128]{1,0:T(8,128)(2,1)S(1)} %collective-permute-done.2.rest_2_), channel_id=1, source_target_pairs={{0,1},{1,0},{2,3},{3,2},{4,5},{5,4},{6,7},{7,6},{8,9},{9,8},{10,11... | collective-permute-start | bytes 786440 | tf_op jit(solution)/shard_map/ppermute | solution.py:182
  24.8 6.8 %copy-start.2 = (bf16[1024,128]{1,0:T(8,128)(2,1)}, bf16[1024,128]{1,0:T(8,128)(2,1)S(1)}, u32[]{:S(2)}) copy-start(bf16[1024,128]{1,0:T(8,128)(2,1)S(1)} %collective-permute-done.1.rest_1_) | copy-start | bytes 786436
  24.8 6.1 %collective-permute-start.5 = (bf16[1024,128]{1,0:T(8,128)(2,1)S(1)}, bf16[1024,128]{1,0:T(8,128)(2,1)S(1)}, u32[]{:S(2)}, u32[]{:S(2)}) collective-permute-start(bf16[1024,128]{1,0:T(8,128)(2,1)S(1)} %collective-permute-done.1.rest_1_), channel_id=1, source_target_pairs={{0,1},{1,0},{2,3},{3,2},{4,5},{5,4},{6,7},{7,6},{8,9},{9,8},{10,11... | collective-permute-start | bytes 786440 | tf_op jit(solution)/shard_map/ppermute | solution.py:182
  30.1 1.6 %copy-start.3 = (bf16[1024,128]{1,0:T(8,128)(2,1)}, bf16[1024,128]{1,0:T(8,128)(2,1)S(1)}, u32[]{:S(2)}) copy-start(bf16[1024,128]{1,0:T(8,128)(2,1)S(1)} %collective-permute-done.rest_0_) | copy-start | bytes 786436
  30.1 1.5 %collective-permute-start.4 = (bf16[1024,128]{1,0:T(8,128)(2,1)S(1)}, bf16[1024,128]{1,0:T(8,128)(2,1)S(1)}, u32[]{:S(2)}, u32[]{:S(2)}) collective-permute-start(bf16[1024,128]{1,0:T(8,128)(2,1)S(1)} %collective-permute-done.rest_0_), channel_id=1, source_target_pairs={{0,1},{1,0},{2,3},{3,2},{4,5},{5,4},{6,7},{7,6},{8,9},{9,8},{10,11... | collective-permute-start | bytes 786440 | tf_op jit(solution)/shard_map/ppermute | solution.py:182
  30.1 1.6 %copy-start.8 = (s32[1024]{0:T(1024)}, s32[1024]{0:T(1024)S(1)}, u32[]{:S(2)}) copy-start(s32[1024]{0:T(1024)S(1)} %broadcast_subtract_fusion) | copy-start | bytes 12292
  30.8 0.8 copy-start.4
  30.9 0.8 copy-start.5
  30.9 0.9 copy-start.6
  31.6 0.7 copy-start.7
  50.4 3.3 %collective-permute-start.8 = (bf16[5,2,256,256]{3,2,1,0:T(8,128)(2,1)}, bf16[5,2,256,256]{3,2,1,0:T(8,128)(2,1)S(1)}, u32[]{:S(2)}, u32[]{:S(2)}) collective-permute-start(bf16[5,2,256,256]{3,2,1,0:T(8,128)(2,1)} %get-tuple-element.11), channel_id=1, source_target_pairs={{0,1},{1,0},{2,3},{3,2},{4,5},{5,4},{6,7},{7,6},{8,9},{9,8},{10,11... | collective-permute-start | bytes 3932168 | tf_op jit(solution)/shard_map/ppermute | solution.py:182
  55.2 37.2 %collective-permute-start.9 = (bf16[2,256,256]{2,1,0:T(8,128)(2,1)S(1)}, bf16[2,256,256]{2,1,0:T(8,128)(2,1)S(1)}, u32[]{:S(2)}, u32[]{:S(2)}) collective-permute-start(bf16[2,256,256]{2,1,0:T(8,128)(2,1)S(1)} %get-tuple-element.12), channel_id=1, source_target_pairs={{0,124},{4,0},{8,4},{12,8},{16,12},{20,16},{24,20},{28,24},{32,28}... | collective-permute-start | bytes 786440 | tf_op jit(solution)/shard_map/ppermute | solution.py:178
  81.6 16.3 %collective-permute-start.12 = (bf16[2,256,256]{2,1,0:T(8,128)(2,1)S(1)}, bf16[2,256,256]{2,1,0:T(8,128)(2,1)S(1)}, u32[]{:S(2)}, u32[]{:S(2)}) collective-permute-start(bf16[2,256,256]{2,1,0:T(8,128)(2,1)S(1)} %get-tuple-element.13), channel_id=1, source_target_pairs={{0,112},{4,116},{8,120},{12,124},{16,0},{20,4},{24,8},{28,12},{32,... | collective-permute-start | bytes 786440 | tf_op jit(solution)/shard_map/ppermute | solution.py:178
  81.6 22.0 %collective-permute-start.11 = (bf16[2,256,256]{2,1,0:T(8,128)(2,1)S(1)}, bf16[2,256,256]{2,1,0:T(8,128)(2,1)S(1)}, u32[]{:S(2)}, u32[]{:S(2)}) collective-permute-start(bf16[2,256,256]{2,1,0:T(8,128)(2,1)S(1)} %get-tuple-element.14), channel_id=1, source_target_pairs={{0,116},{4,120},{8,124},{12,0},{16,4},{20,8},{24,12},{28,16},{32,2... | collective-permute-start | bytes 786440 | tf_op jit(solution)/shard_map/ppermute | solution.py:178
  81.6 26.7 %collective-permute-start.10 = (bf16[2,256,256]{2,1,0:T(8,128)(2,1)S(1)}, bf16[2,256,256]{2,1,0:T(8,128)(2,1)S(1)}, u32[]{:S(2)}, u32[]{:S(2)}) collective-permute-start(bf16[2,256,256]{2,1,0:T(8,128)(2,1)S(1)} %get-tuple-element.15), channel_id=1, source_target_pairs={{0,120},{4,124},{8,0},{12,4},{16,8},{20,12},{24,16},{28,20},{32,24... | collective-permute-start | bytes 786440 | tf_op jit(solution)/shard_map/ppermute | solution.py:178
  109.6 6.6 %collective-permute-start.13 = (bf16[256,256]{1,0:T(8,128)(2,1)S(1)}, bf16[256,256]{1,0:T(8,128)(2,1)S(1)}, u32[]{:S(2)}, u32[]{:S(2)}) collective-permute-start(bf16[256,256]{1,0:T(8,128)(2,1)S(1)} %fusion.8), channel_id=1, source_target_pairs={{0,2},{1,3},{2,0},{3,1},{4,6},{5,7},{6,4},{7,5},{8,10},{9,11},{10,... | collective-permute-start | bytes 393224 | tf_op jit(solution)/shard_map/ppermute | solution.py:182
